TPU v7x, 512 devices: a whole 4x8x8 slice. The times are simulated.
512 devices in a mesh: row: 32 (over y, x), col: 16 (over z, core).
Axes of the slice: x: 4, y: 8, z: 8, core: 2. Of those that a mesh axis runs over, the one named last changes fastest.
Arguments:
- blocks: bfloat16 [32, 16, 2, 8, 128, 128], P('row', 'col'), may hold values from -4 to 4
- block_rows: int32 [32, 16, 2, 8], P('row', 'col'), may hold values from 0 to 4, as said below
- block_cols: int32 [32, 16, 2, 8], P('row', 'col'), may hold values from 0 to 4, as said below
- counts: int32 [32, 16, 2], P('row', 'col'), may hold values from 2 to 8, as said below
Outputs:
- square: bfloat16 [20480, 20480], P('row', 'col')
- trace_value: float32 [], replicated
Inputs may be any that keep to these rules, and one draw needn't show every extreme that they name: `block_rows`: in every (row panel, column panel, group) the 8 slots name distinct block positions; a slot holds data only if its index is below the group's count. `block_cols`: together with block_rows each slot names a distinct position of the 5 x 5 grid of its group. `counts`: some group is full in every draw.
All inputs are finite; a program needn't handle non-finite values.
Results may differ from a plain program's by a relative error of at most 0.001.
Values may be sent and summed in bfloat16 or wider, within the bound.
A program may use at most 64 MiB of HBM per device.

v0:
```python
import math
import jax
import jax.numpy as jnp
from jax import lax
from jax.sharding import PartitionSpec as P

RB = 5
STEPS = 4


def as_sent(shard):
    return jax.tree.map(lambda a: a.astype(jnp.bfloat16) if a.dtype == jnp.float32 else a, shard)


def passed_along(block, axis, distance):
    devices = range(lax.axis_size(axis))
    route = [((i - distance) % len(devices), i) for i in devices]
    return lax.ppermute(block, axis, route)


def densify(pieces, rows, cols, nrows, ncols):
    width = pieces.shape[-1]
    count = pieces.shape[0]
    places = rows * ncols + cols
    onehot = (places[None, :] == jnp.arange(nrows * ncols, dtype=jnp.int32)[:, None]).astype(
        pieces.dtype
    )
    dense = jnp.dot(
        onehot, pieces.reshape(count, width * width), preferred_element_type=jnp.float32
    )
    dense = dense.reshape(nrows, ncols, width, width).transpose(0, 2, 1, 3)
    return dense.reshape(nrows * width, ncols * width).astype(pieces.dtype)


def pick(flag, kept, moved):
    return jax.tree.map(lambda first, second: jnp.where(flag, second, first), kept, moved)


def body(blocks, block_rows, block_cols, counts):
    groups = blocks.shape[2]
    slot_count = blocks.shape[3]
    width = blocks.shape[4]
    row_count = lax.axis_size("row")
    col_count = lax.axis_size("col")
    row_place = lax.axis_index("row")
    col_place = lax.axis_index("col")
    upper = row_place // groups
    lower = row_place % groups
    filled = counts[0, 0]
    live = jnp.arange(slot_count, dtype=jnp.int32)[None, :] < filled[:, None]
    masked = blocks[0, 0] * live[..., None, None].astype(blocks.dtype)
    rows_here = block_rows[0, 0]
    offsets = (jnp.arange(groups, dtype=jnp.int32) * RB)[:, None]
    cols_here = block_cols[0, 0] + offsets
    left_pieces = lax.dynamic_index_in_dim(masked, lower, 0, keepdims=False)
    left_rows = lax.dynamic_index_in_dim(rows_here, lower, 0, keepdims=False)
    left_cols = lax.dynamic_index_in_dim(block_cols[0, 0], lower, 0, keepdims=False)
    left = (left_pieces, left_rows, left_cols)
    right = (masked, rows_here, cols_here)
    left_move = (col_count - upper % col_count) % col_count
    for bit in range((col_count - 1).bit_length()):
        moved = jax.tree.map(
            lambda part, own: part.astype(own.dtype),
            passed_along(as_sent(left), "col", 1 << bit),
            left,
        )
        left = pick(left_move >> bit & 1 == 1, left, moved)
    right_move = (row_count - groups * col_place % row_count) % row_count
    for bit in range((row_count - 1).bit_length()):
        moved = jax.tree.map(
            lambda part, own: part.astype(own.dtype),
            passed_along(as_sent(right), "row", 1 << bit),
            right,
        )
        right = pick(right_move >> bit & 1 == 1, right, moved)
    totals = jnp.zeros((RB * width, groups * RB * width), jnp.float32)
    for step in range(STEPS):
        if step > 0:
            left = jax.tree.map(
                lambda part, own: part.astype(own.dtype),
                passed_along(as_sent(left), "col", col_count - 1),
                left,
            )
            right = jax.tree.map(
                lambda part, own: part.astype(own.dtype),
                passed_along(as_sent(right), "row", row_count - groups),
                right,
            )
        right_dense = densify(
            right[0].reshape(groups * slot_count, width, width),
            right[1].reshape(-1),
            right[2].reshape(-1),
            RB,
            groups * RB,
        )
        left_dense = densify(left[0], left[1], left[2], RB, RB)
        totals = totals + jnp.dot(left_dense, right_dense, preferred_element_type=jnp.float32)
    shift_amount = row_place - groups * col_place
    valid = (shift_amount >= 0) & (shift_amount < groups)
    start = jnp.clip(shift_amount, 0, groups - 1) * RB * width
    window = lax.dynamic_slice_in_dim(totals, start, RB * width, 1)
    term = jnp.where(valid, jnp.trace(window), jnp.zeros((), jnp.float32))
    overall = lax.psum(term, ("row", "col"))
    trace_value = overall / math.sqrt(row_count * RB * width)
    return (totals.astype(jnp.bfloat16), trace_value)


def solution(mesh):
    return jax.shard_map(
        body,
        mesh=mesh,
        in_specs=(
            P("row", "col", None, None, None, None),
            P("row", "col", None, None),
            P("row", "col", None, None),
            P("row", "col", None),
        ),
        out_specs=(P("row", "col"), P()),
        check_vma=False,
    )
```

profile of v0, /device:TPU:1, one launch (start us, length us, event | category | flops | bytes accessed | tf_op | source)
XLA Modules:
  0.0 380.4 jit_solution(16158533486816690697)
XLA Ops:
  0.6 4.1 %collective-permute-start.12 = (s32[2,8]{1,0:T(2,128)}, s32[2,8]{1,0:T(2,128)S(1)}, u32[]{:S(2)}, u32[]{:S(2)}) collective-permute-start(s32[2,8]{1,0:T(2,128)} %bitcast.239), channel_id=1, source_target_pairs={{496,0},{0,16},{16,32},{32,48},{48,64},{64,80},{80,96},{96,112},{1... | collective-permute-start | bytes 200 | tf_op jit(solution)/shard_map/ppermute | solution.py:18
  5.5 3.1 collective-permute-start.17
  13.4 3.5 collective-permute-start.8
  23.4 3.9 %collective-permute-done.4 = s32[8]{0:T(128)S(1)} collective-permute-done((s32[8]{0:T(128)S(1)}, s32[8]{0:T(128)S(1)}, u32[]{:S(2)}, u32[]{:S(2)}) %collective-permute-start.4) | collective-permute-done | bytes 64 | tf_op jit(solution)/shard_map/ppermute | solution.py:18
  32.8 4.6 %collective-permute-start.13 = (s32[2,8]{1,0:T(2,128)S(1)}, s32[2,8]{1,0:T(2,128)S(1)}, u32[]{:S(2)}, u32[]{:S(2)}) collective-permute-start(s32[2,8]{1,0:T(2,128)S(1)} %broadcast_select_fusion.10), channel_id=1, source_target_pairs={{480,0},{496,16},{0,32},{16,48},{32,64},{48,80},{64,96},{80,112},{... | collective-permute-start | bytes 200 | tf_op jit(solution)/shard_map/ppermute | solution.py:18
  38.2 3.1 collective-permute-start.18
  41.4 6.2 %collective-permute-start.2 = (s32[8]{0:T(128)S(1)}, s32[8]{0:T(128)S(1)}, u32[]{:S(2)}, u32[]{:S(2)}) collective-permute-start(s32[8]{0:T(128)S(1)} %broadcast_select_fusion.22), channel_id=1, source_target_pairs={{12,0},{13,1},{14,2},{15,3},{0,4},{1,5},{2,6},{3,7},{4,8},{5,9},{6... | collective-permute-start | bytes 104 | tf_op jit(solution)/shard_map/ppermute | solution.py:18
  48.3 4.5 %collective-permute-start.6 = (s32[8]{0:T(128)S(1)}, s32[8]{0:T(128)S(1)}, u32[]{:S(2)}, u32[]{:S(2)}) collective-permute-start(s32[8]{0:T(128)S(1)} %broadcast_select_fusion.21), channel_id=1, source_target_pairs={{12,0},{13,1},{14,2},{15,3},{0,4},{1,5},{2,6},{3,7},{4,8},{5,9},{6... | collective-permute-start | bytes 104 | tf_op jit(solution)/shard_map/ppermute | solution.py:18
  54.7 7.5 %collective-permute-start.3 = (s32[8]{0:T(128)S(1)}, s32[8]{0:T(128)S(1)}, u32[]{:S(2)}, u32[]{:S(2)}) collective-permute-start(s32[8]{0:T(128)S(1)} %broadcast_select_fusion.24), channel_id=1, source_target_pairs={{8,0},{9,1},{10,2},{11,3},{12,4},{13,5},{14,6},{15,7},{0,8},{1,9},... | collective-permute-start | bytes 104 | tf_op jit(solution)/shard_map/ppermute | solution.py:18
  64.1 3.2 collective-permute-start.14
  67.3 3.2 collective-permute-start.19
  70.6 7.6 %collective-permute-start.28 = (s32[8]{0:T(128)S(1)}, s32[8]{0:T(128)S(1)}, u32[]{:S(2)}, u32[]{:S(2)}) collective-permute-start(s32[8]{0:T(128)S(1)} %get-tuple-element.4), channel_id=1, source_target_pairs={{1,0},{2,1},{3,2},{4,3},{5,4},{6,5},{7,6},{8,7},{9,8},{10,9},{11,1... | collective-permute-start | bytes 104 | tf_op jit(solution)/shard_map/ppermute | solution.py:18
  86.6 4.5 %collective-permute-start.15 = (s32[2,8]{1,0:T(2,128)S(1)}, s32[2,8]{1,0:T(2,128)S(1)}, u32[]{:S(2)}, u32[]{:S(2)}) collective-permute-start(s32[2,8]{1,0:T(2,128)S(1)} %broadcast_select_fusion.14), channel_id=1, source_target_pairs={{384,0},{400,16},{416,32},{432,48},{448,64},{464,80},{480,96},{496... | collective-permute-start | bytes 200 | tf_op jit(solution)/shard_map/ppermute | solution.py:18
  99.5 4.4 %collective-permute-start.16 = (s32[2,8]{1,0:T(2,128)S(1)}, s32[2,8]{1,0:T(2,128)S(1)}, u32[]{:S(2)}, u32[]{:S(2)}) collective-permute-start(s32[2,8]{1,0:T(2,128)S(1)} %broadcast_select_fusion.16), channel_id=1, source_target_pairs={{256,0},{272,16},{288,32},{304,48},{320,64},{336,80},{352,96},{368... | collective-permute-start | bytes 200 | tf_op jit(solution)/shard_map/ppermute | solution.py:18
  104.0 4.8 %collective-permute-start.21 = (s32[2,8]{1,0:T(2,128)S(1)}, s32[2,8]{1,0:T(2,128)S(1)}, u32[]{:S(2)}, u32[]{:S(2)}) collective-permute-start(s32[2,8]{1,0:T(2,128)S(1)} %broadcast_select_fusion.15), channel_id=1, source_target_pairs={{256,0},{272,16},{288,32},{304,48},{320,64},{336,80},{352,96},{368... | collective-permute-start | bytes 200 | tf_op jit(solution)/shard_map/ppermute | solution.py:18
  110.9 3.8 collective-permute-start.23
  114.6 5.4 %collective-permute-done.9 = bf16[8,128,128]{2,1,0:T(8,128)(2,1)S(1)} collective-permute-done((bf16[8,128,128]{2,1,0:T(8,128)(2,1)S(1)}, bf16[8,128,128]{2,1,0:T(8,128)(2,1)S(1)}, u32[]{:S(2)}, u32[]{:S(2)}) %collective-permute-start.9) | collective-permute-done | bytes 262176 | tf_op jit(solution)/shard_map/ppermute | solution.py:18
  122.1 5.7 %collective-permute-start.31 = (s32[2,8]{1,0:T(2,128)S(1)}, s32[2,8]{1,0:T(2,128)S(1)}, u32[]{:S(2)}, u32[]{:S(2)}) collective-permute-start(s32[2,8]{1,0:T(2,128)S(1)} %get-tuple-element.7), channel_id=1, source_target_pairs={{32,0},{48,16},{64,32},{80,48},{96,64},{112,80},{128,96},{144,112}... | collective-permute-start | bytes 200 | tf_op jit(solution)/shard_map/ppermute | solution.py:18
  134.1 4.8 %collective-permute-start.37 = (s32[2,8]{1,0:T(2,128)S(1)}, s32[2,8]{1,0:T(2,128)S(1)}, u32[]{:S(2)}, u32[]{:S(2)}) collective-permute-start(s32[2,8]{1,0:T(2,128)S(1)} %collective-permute-done.31), channel_id=1, source_target_pairs={{32,0},{48,16},{64,32},{80,48},{96,64},{112,80},{128,96},{144,112}... | collective-permute-start | bytes 200 | tf_op jit(solution)/shard_map/ppermute | solution.py:18
  141.7 5.4 %collective-permute-start.11 = (bf16[8,128,128]{2,1,0:T(8,128)(2,1)S(1)}, bf16[8,128,128]{2,1,0:T(8,128)(2,1)S(1)}, u32[]{:S(2)}, u32[]{:S(2)}) collective-permute-start(bf16[8,128,128]{2,1,0:T(8,128)(2,1)S(1)} %broadcast_select_fusion.7), channel_id=1, source_target_pairs={{8,0},{9,1},{10,2},{11,3},{12,4},{13,5},{14,6},{15,7},{0,8},{1,9},... | collective-permute-start | bytes 786440 | tf_op jit(solution)/shard_map/ppermute | solution.py:18
  149.6 6.0 %collective-permute-start.43 = (s32[2,8]{1,0:T(2,128)S(1)}, s32[2,8]{1,0:T(2,128)S(1)}, u32[]{:S(2)}, u32[]{:S(2)}) collective-permute-start(s32[2,8]{1,0:T(2,128)S(1)} %collective-permute-done.37), channel_id=1, source_target_pairs={{32,0},{48,16},{64,32},{80,48},{96,64},{112,80},{128,96},{144,112}... | collective-permute-start | bytes 200 | tf_op jit(solution)/shard_map/ppermute | solution.py:18
  161.6 5.6 %collective-permute-start.29 = (bf16[8,128,128]{2,1,0:T(8,128)(2,1)S(1)}, bf16[8,128,128]{2,1,0:T(8,128)(2,1)S(1)}, u32[]{:S(2)}, u32[]{:S(2)}) collective-permute-start(bf16[8,128,128]{2,1,0:T(8,128)(2,1)S(1)} %broadcast_select_fusion.8), channel_id=1, source_target_pairs={{1,0},{2,1},{3,2},{4,3},{5,4},{6,5},{7,6},{8,7},{9,8},{10,9},{11,1... | collective-permute-start | bytes 786440 | tf_op jit(solution)/shard_map/ppermute | solution.py:18
  171.7 4.9 %collective-permute-done.35 = bf16[8,128,128]{2,1,0:T(8,128)(2,1)S(1)} collective-permute-done((bf16[8,128,128]{2,1,0:T(8,128)(2,1)S(1)}, bf16[8,128,128]{2,1,0:T(8,128)(2,1)S(1)}, u32[]{:S(2)}, u32[]{:S(2)}) %collective-permute-start.35) | collective-permute-done | bytes 262176 | tf_op jit(solution)/shard_map/ppermute | solution.py:18
  178.2 15.1 %collective-permute-done.25 = bf16[2,8,128,128]{3,2,1,0:T(8,128)(2,1)S(1)} collective-permute-done((bf16[2,8,128,128]{3,2,1,0:T(8,128)(2,1)S(1)}, bf16[2,8,128,128]{3,2,1,0:T(8,128)(2,1)S(1)}, u32[]{:S(2)}, u32[]{:S(2)}) %collective-permute-start.25) | collective-permute-done | bytes 524320 | tf_op jit(solution)/shard_map/ppermute | solution.py:18
  193.4 4.2 %collective-permute-start.26 = (bf16[2,8,128,128]{3,2,1,0:T(8,128)(2,1)S(1)}, bf16[2,8,128,128]{3,2,1,0:T(8,128)(2,1)S(1)}, u32[]{:S(2)}, u32[]{:S(2)}) collective-permute-start(bf16[2,8,128,128]{3,2,1,0:T(8,128)(2,1)S(1)} %broadcast_select_fusion.3), channel_id=1, source_target_pairs={{256,0},{272,16},{288,32},{304,48},{320,64},{336,80},{352,96},{368... | collective-permute-start | bytes 1572872 | tf_op jit(solution)/shard_map/ppermute | solution.py:18
  198.6 25.7 %collective-permute-done.26 = bf16[2,8,128,128]{3,2,1,0:T(8,128)(2,1)S(1)} collective-permute-done((bf16[2,8,128,128]{3,2,1,0:T(8,128)(2,1)S(1)}, bf16[2,8,128,128]{3,2,1,0:T(8,128)(2,1)S(1)}, u32[]{:S(2)}, u32[]{:S(2)}) %collective-permute-start.26) | collective-permute-done | bytes 524320 | tf_op jit(solution)/shard_map/ppermute | solution.py:18
  228.7 12.0 %collective-permute-done.32 = bf16[2,8,128,128]{3,2,1,0:T(8,128)(2,1)S(1)} collective-permute-done((bf16[2,8,128,128]{3,2,1,0:T(8,128)(2,1)S(1)}, bf16[2,8,128,128]{3,2,1,0:T(8,128)(2,1)S(1)}, u32[]{:S(2)}, u32[]{:S(2)}) %collective-permute-start.32) | collective-permute-done | bytes 524320 | tf_op jit(solution)/shard_map/ppermute | solution.py:18
  240.7 4.3 %collective-permute-start.38 = (bf16[2,8,128,128]{3,2,1,0:T(8,128)(2,1)S(1)}, bf16[2,8,128,128]{3,2,1,0:T(8,128)(2,1)S(1)}, u32[]{:S(2)}, u32[]{:S(2)}) collective-permute-start(bf16[2,8,128,128]{3,2,1,0:T(8,128)(2,1)S(1)} %collective-permute-done.32), channel_id=1, source_target_pairs={{32,0},{48,16},{64,32},{80,48},{96,64},{112,80},{128,96},{144,112}... | collective-permute-start | bytes 1572872 | tf_op jit(solution)/shard_map/ppermute | solution.py:18
  247.4 8.7 %collective-permute-done.38 = bf16[2,8,128,128]{3,2,1,0:T(8,128)(2,1)S(1)} collective-permute-done((bf16[2,8,128,128]{3,2,1,0:T(8,128)(2,1)S(1)}, bf16[2,8,128,128]{3,2,1,0:T(8,128)(2,1)S(1)}, u32[]{:S(2)}, u32[]{:S(2)}) %collective-permute-start.38) | collective-permute-done | bytes 524320 | tf_op jit(solution)/shard_map/ppermute | solution.py:18
  256.1 6.9 %collective-permute-start.44 = (bf16[2,8,128,128]{3,2,1,0:T(8,128)(2,1)S(1)}, bf16[2,8,128,128]{3,2,1,0:T(8,128)(2,1)S(1)}, u32[]{:S(2)}, u32[]{:S(2)}) collective-permute-start(bf16[2,8,128,128]{3,2,1,0:T(8,128)(2,1)S(1)} %collective-permute-done.38), channel_id=1, source_target_pairs={{32,0},{48,16},{64,32},{80,48},{96,64},{112,80},{128,96},{144,112}... | collective-permute-start | bytes 1572872 | tf_op jit(solution)/shard_map/ppermute | solution.py:18
  265.4 6.6 %collective-permute-done.44 = bf16[2,8,128,128]{3,2,1,0:T(8,128)(2,1)S(1)} collective-permute-done((bf16[2,8,128,128]{3,2,1,0:T(8,128)(2,1)S(1)}, bf16[2,8,128,128]{3,2,1,0:T(8,128)(2,1)S(1)}, u32[]{:S(2)}, u32[]{:S(2)}) %collective-permute-start.44) | collective-permute-done | bytes 524320 | tf_op jit(solution)/shard_map/ppermute | solution.py:18
  277.0 101.6 %psum.7 = f32[]{:T(128)} all-reduce(f32[]{:T(128)S(6)} %select_n.252), channel_id=1, replica_groups=mesh['row'=32,'col'=16] {'row','col'}, use_global_device_ids=true, to_apply=%region_1.2 | all-reduce | flops 1 | bytes 8 | tf_op jit(solution)/shard_map/psum | solution.py:103
  (118 shorter events, 81.4 us)
Async XLA Ops:
  0.6 29.2 %collective-permute-start.12 = (s32[2,8]{1,0:T(2,128)}, s32[2,8]{1,0:T(2,128)S(1)}, u32[]{:S(2)}, u32[]{:S(2)}) collective-permute-start(s32[2,8]{1,0:T(2,128)} %bitcast.239), channel_id=1, source_target_pairs={{496,0},{0,16},{16,32},{32,48},{48,64},{64,80},{80,96},{96,112},{1... | collective-permute-start | bytes 200 | tf_op jit(solution)/shard_map/ppermute | solution.py:18
  5.5 27.3 %collective-permute-start.17 = (s32[2,8]{1,0:T(2,128)S(1)}, s32[2,8]{1,0:T(2,128)S(1)}, u32[]{:S(2)}, u32[]{:S(2)}) collective-permute-start(s32[2,8]{1,0:T(2,128)S(1)} %bitcast_add_fusion), channel_id=1, source_target_pairs={{496,0},{0,16},{16,32},{32,48},{48,64},{64,80},{80,96},{96,112},{1... | collective-permute-start | bytes 200 | tf_op jit(solution)/shard_map/ppermute | solution.py:18
  10.5 100.3 %collective-permute-start.22 = (bf16[2,8,128,128]{3,2,1,0:T(8,128)(2,1)S(1)}, bf16[2,8,128,128]{3,2,1,0:T(8,128)(2,1)S(1)}, u32[]{:S(2)}, u32[]{:S(2)}) collective-permute-start(bf16[2,8,128,128]{3,2,1,0:T(8,128)(2,1)S(1)} %bitcast_multiply_fusion), channel_id=1, source_target_pairs={{496,0},{0,16},{16,32},{32,48},{48,64},{64,80},{80,96},{96,112},{1... | collective-permute-start | bytes 1572872 | tf_op jit(solution)/shard_map/ppermute | solution.py:18
  13.4 95.4 %collective-permute-start.8 = (bf16[8,128,128]{2,1,0:T(8,128)(2,1)S(1)}, bf16[8,128,128]{2,1,0:T(8,128)(2,1)S(1)}, u32[]{:S(2)}, u32[]{:S(2)}) collective-permute-start(bf16[8,128,128]{2,1,0:T(8,128)(2,1)S(1)} %dynamic-slice_bitcast_fusion), channel_id=1, source_target_pairs={{15,0},{0,1},{1,2},{2,3},{3,4},{4,5},{5,6},{6,7},{7,8},{8,9},{9,10... | collective-permute-start | bytes 786440 | tf_op jit(solution)/shard_map/ppermute | solution.py:18
  27.3 11.0 %collective-permute-start.1 = (s32[8]{0:T(128)S(1)}, s32[8]{0:T(128)S(1)}, u32[]{:S(2)}, u32[]{:S(2)}) collective-permute-start(s32[8]{0:T(128)S(1)} %broadcast_select_fusion.20), channel_id=1, source_target_pairs={{14,0},{15,1},{0,2},{1,3},{2,4},{3,5},{4,6},{5,7},{6,8},{7,9},{8,1... | collective-permute-start | bytes 104 | tf_op jit(solution)/shard_map/ppermute | solution.py:18
  29.9 11.5 %collective-permute-start.5 = (s32[8]{0:T(128)S(1)}, s32[8]{0:T(128)S(1)}, u32[]{:S(2)}, u32[]{:S(2)}) collective-permute-start(s32[8]{0:T(128)S(1)} %broadcast_select_fusion.19), channel_id=1, source_target_pairs={{14,0},{15,1},{0,2},{1,3},{2,4},{3,5},{4,6},{5,7},{6,8},{7,9},{8,1... | collective-permute-start | bytes 104 | tf_op jit(solution)/shard_map/ppermute | solution.py:18
  32.8 29.3 %collective-permute-start.13 = (s32[2,8]{1,0:T(2,128)S(1)}, s32[2,8]{1,0:T(2,128)S(1)}, u32[]{:S(2)}, u32[]{:S(2)}) collective-permute-start(s32[2,8]{1,0:T(2,128)S(1)} %broadcast_select_fusion.10), channel_id=1, source_target_pairs={{480,0},{496,16},{0,32},{16,48},{32,64},{48,80},{64,96},{80,112},{... | collective-permute-start | bytes 200 | tf_op jit(solution)/shard_map/ppermute | solution.py:18
  38.2 25.8 %collective-permute-start.18 = (s32[2,8]{1,0:T(2,128)S(1)}, s32[2,8]{1,0:T(2,128)S(1)}, u32[]{:S(2)}, u32[]{:S(2)}) collective-permute-start(s32[2,8]{1,0:T(2,128)S(1)} %broadcast_select_fusion.9), channel_id=1, source_target_pairs={{480,0},{496,16},{0,32},{16,48},{32,64},{48,80},{64,96},{80,112},{... | collective-permute-start | bytes 200 | tf_op jit(solution)/shard_map/ppermute | solution.py:18
  54.7 12.7 %collective-permute-start.3 = (s32[8]{0:T(128)S(1)}, s32[8]{0:T(128)S(1)}, u32[]{:S(2)}, u32[]{:S(2)}) collective-permute-start(s32[8]{0:T(128)S(1)} %broadcast_select_fusion.24), channel_id=1, source_target_pairs={{8,0},{9,1},{10,2},{11,3},{12,4},{13,5},{14,6},{15,7},{0,8},{1,9},... | collective-permute-start | bytes 104 | tf_op jit(solution)/shard_map/ppermute | solution.py:18
  64.1 19.6 %collective-permute-start.14 = (s32[2,8]{1,0:T(2,128)S(1)}, s32[2,8]{1,0:T(2,128)S(1)}, u32[]{:S(2)}, u32[]{:S(2)}) collective-permute-start(s32[2,8]{1,0:T(2,128)S(1)} %broadcast_select_fusion.12), channel_id=1, source_target_pairs={{448,0},{464,16},{480,32},{496,48},{0,64},{16,80},{32,96},{48,112}... | collective-permute-start | bytes 200 | tf_op jit(solution)/shard_map/ppermute | solution.py:18
  67.3 19.2 %collective-permute-start.19 = (s32[2,8]{1,0:T(2,128)S(1)}, s32[2,8]{1,0:T(2,128)S(1)}, u32[]{:S(2)}, u32[]{:S(2)}) collective-permute-start(s32[2,8]{1,0:T(2,128)S(1)} %broadcast_select_fusion.11), channel_id=1, source_target_pairs={{448,0},{464,16},{480,32},{496,48},{0,64},{16,80},{32,96},{48,112}... | collective-permute-start | bytes 200 | tf_op jit(solution)/shard_map/ppermute | solution.py:18
  82.0 9.1 %collective-permute-start.34 = (s32[8]{0:T(128)S(1)}, s32[8]{0:T(128)S(1)}, u32[]{:S(2)}, u32[]{:S(2)}) collective-permute-start(s32[8]{0:T(128)S(1)} %collective-permute-done.28), channel_id=1, source_target_pairs={{1,0},{2,1},{3,2},{4,3},{5,4},{6,5},{7,6},{8,7},{9,8},{10,9},{11,1... | collective-permute-start | bytes 104 | tf_op jit(solution)/shard_map/ppermute | solution.py:18
  83.7 9.9 %collective-permute-start.33 = (s32[8]{0:T(128)S(1)}, s32[8]{0:T(128)S(1)}, u32[]{:S(2)}, u32[]{:S(2)}) collective-permute-start(s32[8]{0:T(128)S(1)} %collective-permute-done.27), channel_id=1, source_target_pairs={{1,0},{2,1},{3,2},{4,3},{5,4},{6,5},{7,6},{8,7},{9,8},{10,9},{11,1... | collective-permute-start | bytes 104 | tf_op jit(solution)/shard_map/ppermute | solution.py:18
  86.6 13.0 %collective-permute-start.15 = (s32[2,8]{1,0:T(2,128)S(1)}, s32[2,8]{1,0:T(2,128)S(1)}, u32[]{:S(2)}, u32[]{:S(2)}) collective-permute-start(s32[2,8]{1,0:T(2,128)S(1)} %broadcast_select_fusion.14), channel_id=1, source_target_pairs={{384,0},{400,16},{416,32},{432,48},{448,64},{464,80},{480,96},{496... | collective-permute-start | bytes 200 | tf_op jit(solution)/shard_map/ppermute | solution.py:18
  91.1 12.8 %collective-permute-start.20 = (s32[2,8]{1,0:T(2,128)S(1)}, s32[2,8]{1,0:T(2,128)S(1)}, u32[]{:S(2)}, u32[]{:S(2)}) collective-permute-start(s32[2,8]{1,0:T(2,128)S(1)} %broadcast_select_fusion.13), channel_id=1, source_target_pairs={{384,0},{400,16},{416,32},{432,48},{448,64},{464,80},{480,96},{496... | collective-permute-start | bytes 200 | tf_op jit(solution)/shard_map/ppermute | solution.py:18
  99.5 22.5 %collective-permute-start.16 = (s32[2,8]{1,0:T(2,128)S(1)}, s32[2,8]{1,0:T(2,128)S(1)}, u32[]{:S(2)}, u32[]{:S(2)}) collective-permute-start(s32[2,8]{1,0:T(2,128)S(1)} %broadcast_select_fusion.16), channel_id=1, source_target_pairs={{256,0},{272,16},{288,32},{304,48},{320,64},{336,80},{352,96},{368... | collective-permute-start | bytes 200 | tf_op jit(solution)/shard_map/ppermute | solution.py:18
  104.0 18.1 %collective-permute-start.21 = (s32[2,8]{1,0:T(2,128)S(1)}, s32[2,8]{1,0:T(2,128)S(1)}, u32[]{:S(2)}, u32[]{:S(2)}) collective-permute-start(s32[2,8]{1,0:T(2,128)S(1)} %broadcast_select_fusion.15), channel_id=1, source_target_pairs={{256,0},{272,16},{288,32},{304,48},{320,64},{336,80},{352,96},{368... | collective-permute-start | bytes 200 | tf_op jit(solution)/shard_map/ppermute | solution.py:18
  108.8 11.2 %collective-permute-start.9 = (bf16[8,128,128]{2,1,0:T(8,128)(2,1)S(1)}, bf16[8,128,128]{2,1,0:T(8,128)(2,1)S(1)}, u32[]{:S(2)}, u32[]{:S(2)}) collective-permute-start(bf16[8,128,128]{2,1,0:T(8,128)(2,1)S(1)} %broadcast_select_fusion.5), channel_id=1, source_target_pairs={{14,0},{15,1},{0,2},{1,3},{2,4},{3,5},{4,6},{5,7},{6,8},{7,9},{8,1... | collective-permute-start | bytes 786440 | tf_op jit(solution)/shard_map/ppermute | solution.py:18
  110.9 36.3 %collective-permute-start.23 = (bf16[2,8,128,128]{3,2,1,0:T(8,128)(2,1)S(1)}, bf16[2,8,128,128]{3,2,1,0:T(8,128)(2,1)S(1)}, u32[]{:S(2)}, u32[]{:S(2)}) collective-permute-start(bf16[2,8,128,128]{3,2,1,0:T(8,128)(2,1)S(1)} %broadcast_select_fusion), channel_id=1, source_target_pairs={{480,0},{496,16},{0,32},{16,48},{32,64},{48,80},{64,96},{80,112},{... | collective-permute-start | bytes 1572872 | tf_op jit(solution)/shard_map/ppermute | solution.py:18
  120.1 21.6 %collective-permute-start.10 = (bf16[8,128,128]{2,1,0:T(8,128)(2,1)S(1)}, bf16[8,128,128]{2,1,0:T(8,128)(2,1)S(1)}, u32[]{:S(2)}, u32[]{:S(2)}) collective-permute-start(bf16[8,128,128]{2,1,0:T(8,128)(2,1)S(1)} %broadcast_select_fusion.6), channel_id=1, source_target_pairs={{12,0},{13,1},{14,2},{15,3},{0,4},{1,5},{2,6},{3,7},{4,8},{5,9},{6... | collective-permute-start | bytes 786440 | tf_op jit(solution)/shard_map/ppermute | solution.py:18
  122.1 8.8 %collective-permute-start.31 = (s32[2,8]{1,0:T(2,128)S(1)}, s32[2,8]{1,0:T(2,128)S(1)}, u32[]{:S(2)}, u32[]{:S(2)}) collective-permute-start(s32[2,8]{1,0:T(2,128)S(1)} %get-tuple-element.7), channel_id=1, source_target_pairs={{32,0},{48,16},{64,32},{80,48},{96,64},{112,80},{128,96},{144,112}... | collective-permute-start | bytes 200 | tf_op jit(solution)/shard_map/ppermute | solution.py:18
  134.1 15.5 %collective-permute-start.37 = (s32[2,8]{1,0:T(2,128)S(1)}, s32[2,8]{1,0:T(2,128)S(1)}, u32[]{:S(2)}, u32[]{:S(2)}) collective-permute-start(s32[2,8]{1,0:T(2,128)S(1)} %collective-permute-done.31), channel_id=1, source_target_pairs={{32,0},{48,16},{64,32},{80,48},{96,64},{112,80},{128,96},{144,112}... | collective-permute-start | bytes 200 | tf_op jit(solution)/shard_map/ppermute | solution.py:18
  138.9 10.6 %collective-permute-start.36 = (s32[2,8]{1,0:T(2,128)S(1)}, s32[2,8]{1,0:T(2,128)S(1)}, u32[]{:S(2)}, u32[]{:S(2)}) collective-permute-start(s32[2,8]{1,0:T(2,128)S(1)} %collective-permute-done.30), channel_id=1, source_target_pairs={{32,0},{48,16},{64,32},{80,48},{96,64},{112,80},{128,96},{144,112}... | collective-permute-start | bytes 200 | tf_op jit(solution)/shard_map/ppermute | solution.py:18
  141.7 19.9 %collective-permute-start.11 = (bf16[8,128,128]{2,1,0:T(8,128)(2,1)S(1)}, bf16[8,128,128]{2,1,0:T(8,128)(2,1)S(1)}, u32[]{:S(2)}, u32[]{:S(2)}) collective-permute-start(bf16[8,128,128]{2,1,0:T(8,128)(2,1)S(1)} %broadcast_select_fusion.7), channel_id=1, source_target_pairs={{8,0},{9,1},{10,2},{11,3},{12,4},{13,5},{14,6},{15,7},{0,8},{1,9},... | collective-permute-start | bytes 786440 | tf_op jit(solution)/shard_map/ppermute | solution.py:18
  147.2 20.0 %collective-permute-start.24 = (bf16[2,8,128,128]{3,2,1,0:T(8,128)(2,1)S(1)}, bf16[2,8,128,128]{3,2,1,0:T(8,128)(2,1)S(1)}, u32[]{:S(2)}, u32[]{:S(2)}) collective-permute-start(bf16[2,8,128,128]{3,2,1,0:T(8,128)(2,1)S(1)} %broadcast_select_fusion.1), channel_id=1, source_target_pairs={{448,0},{464,16},{480,32},{496,48},{0,64},{16,80},{32,96},{48,112}... | collective-permute-start | bytes 1572872 | tf_op jit(solution)/shard_map/ppermute | solution.py:18
  161.6 8.8 %collective-permute-start.29 = (bf16[8,128,128]{2,1,0:T(8,128)(2,1)S(1)}, bf16[8,128,128]{2,1,0:T(8,128)(2,1)S(1)}, u32[]{:S(2)}, u32[]{:S(2)}) collective-permute-start(bf16[8,128,128]{2,1,0:T(8,128)(2,1)S(1)} %broadcast_select_fusion.8), channel_id=1, source_target_pairs={{1,0},{2,1},{3,2},{4,3},{5,4},{6,5},{7,6},{8,7},{9,8},{10,9},{11,1... | collective-permute-start | bytes 786440 | tf_op jit(solution)/shard_map/ppermute | solution.py:18
  167.3 26.0 %collective-permute-start.25 = (bf16[2,8,128,128]{3,2,1,0:T(8,128)(2,1)S(1)}, bf16[2,8,128,128]{3,2,1,0:T(8,128)(2,1)S(1)}, u32[]{:S(2)}, u32[]{:S(2)}) collective-permute-start(bf16[2,8,128,128]{3,2,1,0:T(8,128)(2,1)S(1)} %broadcast_select_fusion.2), channel_id=1, source_target_pairs={{384,0},{400,16},{416,32},{432,48},{448,64},{464,80},{480,96},{496... | collective-permute-start | bytes 1572872 | tf_op jit(solution)/shard_map/ppermute | solution.py:18
  176.6 21.5 %collective-permute-start.41 = (bf16[8,128,128]{2,1,0:T(8,128)(2,1)S(1)}, bf16[8,128,128]{2,1,0:T(8,128)(2,1)S(1)}, u32[]{:S(2)}, u32[]{:S(2)}) collective-permute-start(bf16[8,128,128]{2,1,0:T(8,128)(2,1)S(1)} %collective-permute-done.35), channel_id=1, source_target_pairs={{1,0},{2,1},{3,2},{4,3},{5,4},{6,5},{7,6},{8,7},{9,8},{10,9},{11,1... | collective-permute-start | bytes 786440 | tf_op jit(solution)/shard_map/ppermute | solution.py:18
  193.4 30.9 %collective-permute-start.26 = (bf16[2,8,128,128]{3,2,1,0:T(8,128)(2,1)S(1)}, bf16[2,8,128,128]{3,2,1,0:T(8,128)(2,1)S(1)}, u32[]{:S(2)}, u32[]{:S(2)}) collective-permute-start(bf16[2,8,128,128]{3,2,1,0:T(8,128)(2,1)S(1)} %broadcast_select_fusion.3), channel_id=1, source_target_pairs={{256,0},{272,16},{288,32},{304,48},{320,64},{336,80},{352,96},{368... | collective-permute-start | bytes 1572872 | tf_op jit(solution)/shard_map/ppermute | solution.py:18
  224.3 16.3 %collective-permute-start.32 = (bf16[2,8,128,128]{3,2,1,0:T(8,128)(2,1)S(1)}, bf16[2,8,128,128]{3,2,1,0:T(8,128)(2,1)S(1)}, u32[]{:S(2)}, u32[]{:S(2)}) collective-permute-start(bf16[2,8,128,128]{3,2,1,0:T(8,128)(2,1)S(1)} %broadcast_select_fusion.4), channel_id=1, source_target_pairs={{32,0},{48,16},{64,32},{80,48},{96,64},{112,80},{128,96},{144,112}... | collective-permute-start | bytes 1572872 | tf_op jit(solution)/shard_map/ppermute | solution.py:18
  240.7 15.4 %collective-permute-start.38 = (bf16[2,8,128,128]{3,2,1,0:T(8,128)(2,1)S(1)}, bf16[2,8,128,128]{3,2,1,0:T(8,128)(2,1)S(1)}, u32[]{:S(2)}, u32[]{:S(2)}) collective-permute-start(bf16[2,8,128,128]{3,2,1,0:T(8,128)(2,1)S(1)} %collective-permute-done.32), channel_id=1, source_target_pairs={{32,0},{48,16},{64,32},{80,48},{96,64},{112,80},{128,96},{144,112}... | collective-permute-start | bytes 1572872 | tf_op jit(solution)/shard_map/ppermute | solution.py:18
  256.1 16.0 %collective-permute-start.44 = (bf16[2,8,128,128]{3,2,1,0:T(8,128)(2,1)S(1)}, bf16[2,8,128,128]{3,2,1,0:T(8,128)(2,1)S(1)}, u32[]{:S(2)}, u32[]{:S(2)}) collective-permute-start(bf16[2,8,128,128]{3,2,1,0:T(8,128)(2,1)S(1)} %collective-permute-done.38), channel_id=1, source_target_pairs={{32,0},{48,16},{64,32},{80,48},{96,64},{112,80},{128,96},{144,112}... | collective-permute-start | bytes 1572872 | tf_op jit(solution)/shard_map/ppermute | solution.py:18
  (14 other events, 185.6 us)
where the time goes:
time: 382 us; the launch traced here: 380 us
  starting transfers between devices  151 us (40%)
  waiting for transfers between devices  102 us (27%)
  blocking collectives  102 us (27%)
  matrix products  12.7 us (3%)
  other arithmetic  6.7 us (2%)
  between operations  3.84 us (1%)
    ppermute x45, starting transfers between devices, passed_along(): return lax.ppermute(block, axis, route)  151 us
    ppermute x45, waiting for transfers between devices, passed_along(): return lax.ppermute(block, axis, route)  102 us
    psum x1, blocking collectives, body(): overall = lax.psum(term, ('row', 'col'))  102 us
  transfers between devices with their start and end apart: 45, of which 18 were waited for; matrix products, arithmetic and copies ran while one was open for 4% of the time, Pallas kernels for 0%

commit v1 on v0

--- a/solution.py
+++ b/solution.py
@@ -3,6 +3,7 @@
 import jax.numpy as jnp
 from jax import lax
 from jax.sharding import PartitionSpec as P
+from jax.lax import psum
 
 RB = 5
 STEPS = 4
@@ -100,7 +101,8 @@
     start = jnp.clip(shift_amount, 0, groups - 1) * RB * width
     window = lax.dynamic_slice_in_dim(totals, start, RB * width, 1)
     term = jnp.where(valid, jnp.trace(window), jnp.zeros((), jnp.float32))
-    overall = lax.psum(term, ("row", "col"))
+    state_next = psum(term, axis_name="row")
+    overall = psum(state_next, axis_name="col")
     trace_value = overall / math.sqrt(row_count * RB * width)
     return (totals.astype(jnp.bfloat16), trace_value)
 

time: 382 us -> 383 us (level)
    psum x1 -> x2, blocking collectives: 102 us -> 103 us  [the longest x1 63.2 us: body(): state_next = psum(term, axis_name='row')]
where the time goes in v1:
time: 383 us; the launch traced here: 382 us
  starting transfers between devices  151 us (39%)
  blocking collectives  103 us (27%)
  waiting for transfers between devices  102 us (27%)
  matrix products  12.7 us (3%)
  other arithmetic  6.7 us (2%)
  between operations  3.84 us (1%)
    ppermute x45, starting transfers between devices, passed_along(): return lax.ppermute(block, axis, route)  151 us
    ppermute x45, waiting for transfers between devices, passed_along(): return lax.ppermute(block, axis, route)  102 us
    psum x1, blocking collectives, body(): state_next = psum(term, axis_name='row')  63.2 us
    psum x1, blocking collectives, body(): overall = psum(state_next, axis_name='col')  40.2 us
  transfers between devices with their start and end apart: 45, of which 18 were waited for; matrix products, arithmetic and copies ran while one was open for 4% of the time, Pallas kernels for 0%

profile of v1, /device:TPU:1, one launch (start us, length us, event | category | flops | bytes accessed | tf_op | source)
XLA Modules:
  0.0 382.1 jit_solution(10839844568424554019)
XLA Ops:
  0.6 4.1 %collective-permute-start.12 = (s32[2,8]{1,0:T(2,128)}, s32[2,8]{1,0:T(2,128)S(1)}, u32[]{:S(2)}, u32[]{:S(2)}) collective-permute-start(s32[2,8]{1,0:T(2,128)} %bitcast.239), channel_id=1, source_target_pairs={{496,0},{0,16},{16,32},{32,48},{48,64},{64,80},{80,96},{96,112},{1... | collective-permute-start | bytes 200 | tf_op jit(solution)/shard_map/ppermute | solution.py:19
  13.4 3.5 collective-permute-start.8
  23.4 3.9 %collective-permute-done.4 = s32[8]{0:T(128)S(1)} collective-permute-done((s32[8]{0:T(128)S(1)}, s32[8]{0:T(128)S(1)}, u32[]{:S(2)}, u32[]{:S(2)}) %collective-permute-start.4) | collective-permute-done | bytes 64 | tf_op jit(solution)/shard_map/ppermute | solution.py:19
  32.8 4.6 %collective-permute-start.13 = (s32[2,8]{1,0:T(2,128)S(1)}, s32[2,8]{1,0:T(2,128)S(1)}, u32[]{:S(2)}, u32[]{:S(2)}) collective-permute-start(s32[2,8]{1,0:T(2,128)S(1)} %broadcast_select_fusion.10), channel_id=1, source_target_pairs={{480,0},{496,16},{0,32},{16,48},{32,64},{48,80},{64,96},{80,112},{... | collective-permute-start | bytes 200 | tf_op jit(solution)/shard_map/ppermute | solution.py:19
  38.2 3.1 collective-permute-start.18
  41.4 6.2 %collective-permute-start.2 = (s32[8]{0:T(128)S(1)}, s32[8]{0:T(128)S(1)}, u32[]{:S(2)}, u32[]{:S(2)}) collective-permute-start(s32[8]{0:T(128)S(1)} %broadcast_select_fusion.22), channel_id=1, source_target_pairs={{12,0},{13,1},{14,2},{15,3},{0,4},{1,5},{2,6},{3,7},{4,8},{5,9},{6... | collective-permute-start | bytes 104 | tf_op jit(solution)/shard_map/ppermute | solution.py:19
  48.3 4.5 %collective-permute-start.6 = (s32[8]{0:T(128)S(1)}, s32[8]{0:T(128)S(1)}, u32[]{:S(2)}, u32[]{:S(2)}) collective-permute-start(s32[8]{0:T(128)S(1)} %broadcast_select_fusion.21), channel_id=1, source_target_pairs={{12,0},{13,1},{14,2},{15,3},{0,4},{1,5},{2,6},{3,7},{4,8},{5,9},{6... | collective-permute-start | bytes 104 | tf_op jit(solution)/shard_map/ppermute | solution.py:19
  54.7 7.5 %collective-permute-start.3 = (s32[8]{0:T(128)S(1)}, s32[8]{0:T(128)S(1)}, u32[]{:S(2)}, u32[]{:S(2)}) collective-permute-start(s32[8]{0:T(128)S(1)} %broadcast_select_fusion.24), channel_id=1, source_target_pairs={{8,0},{9,1},{10,2},{11,3},{12,4},{13,5},{14,6},{15,7},{0,8},{1,9},... | collective-permute-start | bytes 104 | tf_op jit(solution)/shard_map/ppermute | solution.py:19
  64.1 3.2 collective-permute-start.14
  67.3 3.2 collective-permute-start.19
  70.6 7.6 %collective-permute-start.28 = (s32[8]{0:T(128)S(1)}, s32[8]{0:T(128)S(1)}, u32[]{:S(2)}, u32[]{:S(2)}) collective-permute-start(s32[8]{0:T(128)S(1)} %get-tuple-element.4), channel_id=1, source_target_pairs={{1,0},{2,1},{3,2},{4,3},{5,4},{6,5},{7,6},{8,7},{9,8},{10,9},{11,1... | collective-permute-start | bytes 104 | tf_op jit(solution)/shard_map/ppermute | solution.py:19
  86.6 4.5 %collective-permute-start.15 = (s32[2,8]{1,0:T(2,128)S(1)}, s32[2,8]{1,0:T(2,128)S(1)}, u32[]{:S(2)}, u32[]{:S(2)}) collective-permute-start(s32[2,8]{1,0:T(2,128)S(1)} %broadcast_select_fusion.14), channel_id=1, source_target_pairs={{384,0},{400,16},{416,32},{432,48},{448,64},{464,80},{480,96},{496... | collective-permute-start | bytes 200 | tf_op jit(solution)/shard_map/ppermute | solution.py:19
  99.5 4.4 %collective-permute-start.16 = (s32[2,8]{1,0:T(2,128)S(1)}, s32[2,8]{1,0:T(2,128)S(1)}, u32[]{:S(2)}, u32[]{:S(2)}) collective-permute-start(s32[2,8]{1,0:T(2,128)S(1)} %broadcast_select_fusion.16), channel_id=1, source_target_pairs={{256,0},{272,16},{288,32},{304,48},{320,64},{336,80},{352,96},{368... | collective-permute-start | bytes 200 | tf_op jit(solution)/shard_map/ppermute | solution.py:19
  104.0 4.8 %collective-permute-start.21 = (s32[2,8]{1,0:T(2,128)S(1)}, s32[2,8]{1,0:T(2,128)S(1)}, u32[]{:S(2)}, u32[]{:S(2)}) collective-permute-start(s32[2,8]{1,0:T(2,128)S(1)} %broadcast_select_fusion.15), channel_id=1, source_target_pairs={{256,0},{272,16},{288,32},{304,48},{320,64},{336,80},{352,96},{368... | collective-permute-start | bytes 200 | tf_op jit(solution)/shard_map/ppermute | solution.py:19
  110.9 3.8 collective-permute-start.23
  114.6 5.4 %collective-permute-done.9 = bf16[8,128,128]{2,1,0:T(8,128)(2,1)S(1)} collective-permute-done((bf16[8,128,128]{2,1,0:T(8,128)(2,1)S(1)}, bf16[8,128,128]{2,1,0:T(8,128)(2,1)S(1)}, u32[]{:S(2)}, u32[]{:S(2)}) %collective-permute-start.9) | collective-permute-done | bytes 262176 | tf_op jit(solution)/shard_map/ppermute | solution.py:19
  122.1 5.7 %collective-permute-start.31 = (s32[2,8]{1,0:T(2,128)S(1)}, s32[2,8]{1,0:T(2,128)S(1)}, u32[]{:S(2)}, u32[]{:S(2)}) collective-permute-start(s32[2,8]{1,0:T(2,128)S(1)} %get-tuple-element.7), channel_id=1, source_target_pairs={{32,0},{48,16},{64,32},{80,48},{96,64},{112,80},{128,96},{144,112}... | collective-permute-start | bytes 200 | tf_op jit(solution)/shard_map/ppermute | solution.py:19
  134.1 4.8 %collective-permute-start.37 = (s32[2,8]{1,0:T(2,128)S(1)}, s32[2,8]{1,0:T(2,128)S(1)}, u32[]{:S(2)}, u32[]{:S(2)}) collective-permute-start(s32[2,8]{1,0:T(2,128)S(1)} %collective-permute-done.31), channel_id=1, source_target_pairs={{32,0},{48,16},{64,32},{80,48},{96,64},{112,80},{128,96},{144,112}... | collective-permute-start | bytes 200 | tf_op jit(solution)/shard_map/ppermute | solution.py:19
  141.7 5.4 %collective-permute-start.11 = (bf16[8,128,128]{2,1,0:T(8,128)(2,1)S(1)}, bf16[8,128,128]{2,1,0:T(8,128)(2,1)S(1)}, u32[]{:S(2)}, u32[]{:S(2)}) collective-permute-start(bf16[8,128,128]{2,1,0:T(8,128)(2,1)S(1)} %broadcast_select_fusion.7), channel_id=1, source_target_pairs={{8,0},{9,1},{10,2},{11,3},{12,4},{13,5},{14,6},{15,7},{0,8},{1,9},... | collective-permute-start | bytes 786440 | tf_op jit(solution)/shard_map/ppermute | solution.py:19
  149.6 6.0 %collective-permute-start.43 = (s32[2,8]{1,0:T(2,128)S(1)}, s32[2,8]{1,0:T(2,128)S(1)}, u32[]{:S(2)}, u32[]{:S(2)}) collective-permute-start(s32[2,8]{1,0:T(2,128)S(1)} %collective-permute-done.37), channel_id=1, source_target_pairs={{32,0},{48,16},{64,32},{80,48},{96,64},{112,80},{128,96},{144,112}... | collective-permute-start | bytes 200 | tf_op jit(solution)/shard_map/ppermute | solution.py:19
  161.6 5.6 %collective-permute-start.29 = (bf16[8,128,128]{2,1,0:T(8,128)(2,1)S(1)}, bf16[8,128,128]{2,1,0:T(8,128)(2,1)S(1)}, u32[]{:S(2)}, u32[]{:S(2)}) collective-permute-start(bf16[8,128,128]{2,1,0:T(8,128)(2,1)S(1)} %broadcast_select_fusion.8), channel_id=1, source_target_pairs={{1,0},{2,1},{3,2},{4,3},{5,4},{6,5},{7,6},{8,7},{9,8},{10,9},{11,1... | collective-permute-start | bytes 786440 | tf_op jit(solution)/shard_map/ppermute | solution.py:19
  171.7 4.9 %collective-permute-done.35 = bf16[8,128,128]{2,1,0:T(8,128)(2,1)S(1)} collective-permute-done((bf16[8,128,128]{2,1,0:T(8,128)(2,1)S(1)}, bf16[8,128,128]{2,1,0:T(8,128)(2,1)S(1)}, u32[]{:S(2)}, u32[]{:S(2)}) %collective-permute-start.35) | collective-permute-done | bytes 262176 | tf_op jit(solution)/shard_map/ppermute | solution.py:19
  178.2 15.1 %collective-permute-done.25 = bf16[2,8,128,128]{3,2,1,0:T(8,128)(2,1)S(1)} collective-permute-done((bf16[2,8,128,128]{3,2,1,0:T(8,128)(2,1)S(1)}, bf16[2,8,128,128]{3,2,1,0:T(8,128)(2,1)S(1)}, u32[]{:S(2)}, u32[]{:S(2)}) %collective-permute-start.25) | collective-permute-done | bytes 524320 | tf_op jit(solution)/shard_map/ppermute | solution.py:19
  193.4 4.2 %collective-permute-start.26 = (bf16[2,8,128,128]{3,2,1,0:T(8,128)(2,1)S(1)}, bf16[2,8,128,128]{3,2,1,0:T(8,128)(2,1)S(1)}, u32[]{:S(2)}, u32[]{:S(2)}) collective-permute-start(bf16[2,8,128,128]{3,2,1,0:T(8,128)(2,1)S(1)} %broadcast_select_fusion.3), channel_id=1, source_target_pairs={{256,0},{272,16},{288,32},{304,48},{320,64},{336,80},{352,96},{368... | collective-permute-start | bytes 1572872 | tf_op jit(solution)/shard_map/ppermute | solution.py:19
  198.6 25.7 %collective-permute-done.26 = bf16[2,8,128,128]{3,2,1,0:T(8,128)(2,1)S(1)} collective-permute-done((bf16[2,8,128,128]{3,2,1,0:T(8,128)(2,1)S(1)}, bf16[2,8,128,128]{3,2,1,0:T(8,128)(2,1)S(1)}, u32[]{:S(2)}, u32[]{:S(2)}) %collective-permute-start.26) | collective-permute-done | bytes 524320 | tf_op jit(solution)/shard_map/ppermute | solution.py:19
  228.7 12.0 %collective-permute-done.32 = bf16[2,8,128,128]{3,2,1,0:T(8,128)(2,1)S(1)} collective-permute-done((bf16[2,8,128,128]{3,2,1,0:T(8,128)(2,1)S(1)}, bf16[2,8,128,128]{3,2,1,0:T(8,128)(2,1)S(1)}, u32[]{:S(2)}, u32[]{:S(2)}) %collective-permute-start.32) | collective-permute-done | bytes 524320 | tf_op jit(solution)/shard_map/ppermute | solution.py:19
  240.7 4.3 %collective-permute-start.38 = (bf16[2,8,128,128]{3,2,1,0:T(8,128)(2,1)S(1)}, bf16[2,8,128,128]{3,2,1,0:T(8,128)(2,1)S(1)}, u32[]{:S(2)}, u32[]{:S(2)}) collective-permute-start(bf16[2,8,128,128]{3,2,1,0:T(8,128)(2,1)S(1)} %collective-permute-done.32), channel_id=1, source_target_pairs={{32,0},{48,16},{64,32},{80,48},{96,64},{112,80},{128,96},{144,112}... | collective-permute-start | bytes 1572872 | tf_op jit(solution)/shard_map/ppermute | solution.py:19
  247.4 8.7 %collective-permute-done.38 = bf16[2,8,128,128]{3,2,1,0:T(8,128)(2,1)S(1)} collective-permute-done((bf16[2,8,128,128]{3,2,1,0:T(8,128)(2,1)S(1)}, bf16[2,8,128,128]{3,2,1,0:T(8,128)(2,1)S(1)}, u32[]{:S(2)}, u32[]{:S(2)}) %collective-permute-start.38) | collective-permute-done | bytes 524320 | tf_op jit(solution)/shard_map/ppermute | solution.py:19
  256.1 6.9 %collective-permute-start.44 = (bf16[2,8,128,128]{3,2,1,0:T(8,128)(2,1)S(1)}, bf16[2,8,128,128]{3,2,1,0:T(8,128)(2,1)S(1)}, u32[]{:S(2)}, u32[]{:S(2)}) collective-permute-start(bf16[2,8,128,128]{3,2,1,0:T(8,128)(2,1)S(1)} %collective-permute-done.38), channel_id=1, source_target_pairs={{32,0},{48,16},{64,32},{80,48},{96,64},{112,80},{128,96},{144,112}... | collective-permute-start | bytes 1572872 | tf_op jit(solution)/shard_map/ppermute | solution.py:19
  265.4 6.6 %collective-permute-done.44 = bf16[2,8,128,128]{3,2,1,0:T(8,128)(2,1)S(1)} collective-permute-done((bf16[2,8,128,128]{3,2,1,0:T(8,128)(2,1)S(1)}, bf16[2,8,128,128]{3,2,1,0:T(8,128)(2,1)S(1)}, u32[]{:S(2)}, u32[]{:S(2)}) %collective-permute-start.44) | collective-permute-done | bytes 524320 | tf_op jit(solution)/shard_map/ppermute | solution.py:19
  277.0 63.2 %psum.14 = f32[]{:T(128)} all-reduce(f32[]{:T(128)S(6)} %select_n.252), channel_id=1, replica_groups=mesh['row'=32,'col'=16] {'row'}, use_global_device_ids=true, to_apply=%region_1.2 | all-reduce | flops 1 | bytes 8 | tf_op jit(solution)/shard_map/psum | solution.py:104
  340.2 40.2 %psum.15 = f32[]{:T(128)} all-reduce(f32[]{:T(128)} %psum.14), channel_id=1, replica_groups=mesh['row'=32,'col'=16] {'col'}, use_global_device_ids=true, to_apply=%region_2.3 | all-reduce | flops 1 | bytes 8 | tf_op jit(solution)/shard_map/psum | solution.py:105
  (119 shorter events, 84.5 us)
Async XLA Ops:
  0.6 29.2 %collective-permute-start.12 = (s32[2,8]{1,0:T(2,128)}, s32[2,8]{1,0:T(2,128)S(1)}, u32[]{:S(2)}, u32[]{:S(2)}) collective-permute-start(s32[2,8]{1,0:T(2,128)} %bitcast.239), channel_id=1, source_target_pairs={{496,0},{0,16},{16,32},{32,48},{48,64},{64,80},{80,96},{96,112},{1... | collective-permute-start | bytes 200 | tf_op jit(solution)/shard_map/ppermute | solution.py:19
  5.5 27.3 %collective-permute-start.17 = (s32[2,8]{1,0:T(2,128)S(1)}, s32[2,8]{1,0:T(2,128)S(1)}, u32[]{:S(2)}, u32[]{:S(2)}) collective-permute-start(s32[2,8]{1,0:T(2,128)S(1)} %bitcast_add_fusion), channel_id=1, source_target_pairs={{496,0},{0,16},{16,32},{32,48},{48,64},{64,80},{80,96},{96,112},{1... | collective-permute-start | bytes 200 | tf_op jit(solution)/shard_map/ppermute | solution.py:19
  10.5 100.3 %collective-permute-start.22 = (bf16[2,8,128,128]{3,2,1,0:T(8,128)(2,1)S(1)}, bf16[2,8,128,128]{3,2,1,0:T(8,128)(2,1)S(1)}, u32[]{:S(2)}, u32[]{:S(2)}) collective-permute-start(bf16[2,8,128,128]{3,2,1,0:T(8,128)(2,1)S(1)} %bitcast_multiply_fusion), channel_id=1, source_target_pairs={{496,0},{0,16},{16,32},{32,48},{48,64},{64,80},{80,96},{96,112},{1... | collective-permute-start | bytes 1572872 | tf_op jit(solution)/shard_map/ppermute | solution.py:19
  13.4 95.4 %collective-permute-start.8 = (bf16[8,128,128]{2,1,0:T(8,128)(2,1)S(1)}, bf16[8,128,128]{2,1,0:T(8,128)(2,1)S(1)}, u32[]{:S(2)}, u32[]{:S(2)}) collective-permute-start(bf16[8,128,128]{2,1,0:T(8,128)(2,1)S(1)} %dynamic-slice_bitcast_fusion), channel_id=1, source_target_pairs={{15,0},{0,1},{1,2},{2,3},{3,4},{4,5},{5,6},{6,7},{7,8},{8,9},{9,10... | collective-permute-start | bytes 786440 | tf_op jit(solution)/shard_map/ppermute | solution.py:19
  27.3 11.0 %collective-permute-start.1 = (s32[8]{0:T(128)S(1)}, s32[8]{0:T(128)S(1)}, u32[]{:S(2)}, u32[]{:S(2)}) collective-permute-start(s32[8]{0:T(128)S(1)} %broadcast_select_fusion.20), channel_id=1, source_target_pairs={{14,0},{15,1},{0,2},{1,3},{2,4},{3,5},{4,6},{5,7},{6,8},{7,9},{8,1... | collective-permute-start | bytes 104 | tf_op jit(solution)/shard_map/ppermute | solution.py:19
  29.9 11.5 %collective-permute-start.5 = (s32[8]{0:T(128)S(1)}, s32[8]{0:T(128)S(1)}, u32[]{:S(2)}, u32[]{:S(2)}) collective-permute-start(s32[8]{0:T(128)S(1)} %broadcast_select_fusion.19), channel_id=1, source_target_pairs={{14,0},{15,1},{0,2},{1,3},{2,4},{3,5},{4,6},{5,7},{6,8},{7,9},{8,1... | collective-permute-start | bytes 104 | tf_op jit(solution)/shard_map/ppermute | solution.py:19
  32.8 29.3 %collective-permute-start.13 = (s32[2,8]{1,0:T(2,128)S(1)}, s32[2,8]{1,0:T(2,128)S(1)}, u32[]{:S(2)}, u32[]{:S(2)}) collective-permute-start(s32[2,8]{1,0:T(2,128)S(1)} %broadcast_select_fusion.10), channel_id=1, source_target_pairs={{480,0},{496,16},{0,32},{16,48},{32,64},{48,80},{64,96},{80,112},{... | collective-permute-start | bytes 200 | tf_op jit(solution)/shard_map/ppermute | solution.py:19
  38.2 25.8 %collective-permute-start.18 = (s32[2,8]{1,0:T(2,128)S(1)}, s32[2,8]{1,0:T(2,128)S(1)}, u32[]{:S(2)}, u32[]{:S(2)}) collective-permute-start(s32[2,8]{1,0:T(2,128)S(1)} %broadcast_select_fusion.9), channel_id=1, source_target_pairs={{480,0},{496,16},{0,32},{16,48},{32,64},{48,80},{64,96},{80,112},{... | collective-permute-start | bytes 200 | tf_op jit(solution)/shard_map/ppermute | solution.py:19
  54.7 12.7 %collective-permute-start.3 = (s32[8]{0:T(128)S(1)}, s32[8]{0:T(128)S(1)}, u32[]{:S(2)}, u32[]{:S(2)}) collective-permute-start(s32[8]{0:T(128)S(1)} %broadcast_select_fusion.24), channel_id=1, source_target_pairs={{8,0},{9,1},{10,2},{11,3},{12,4},{13,5},{14,6},{15,7},{0,8},{1,9},... | collective-permute-start | bytes 104 | tf_op jit(solution)/shard_map/ppermute | solution.py:19
  64.1 19.6 %collective-permute-start.14 = (s32[2,8]{1,0:T(2,128)S(1)}, s32[2,8]{1,0:T(2,128)S(1)}, u32[]{:S(2)}, u32[]{:S(2)}) collective-permute-start(s32[2,8]{1,0:T(2,128)S(1)} %broadcast_select_fusion.12), channel_id=1, source_target_pairs={{448,0},{464,16},{480,32},{496,48},{0,64},{16,80},{32,96},{48,112}... | collective-permute-start | bytes 200 | tf_op jit(solution)/shard_map/ppermute | solution.py:19
  67.3 19.2 %collective-permute-start.19 = (s32[2,8]{1,0:T(2,128)S(1)}, s32[2,8]{1,0:T(2,128)S(1)}, u32[]{:S(2)}, u32[]{:S(2)}) collective-permute-start(s32[2,8]{1,0:T(2,128)S(1)} %broadcast_select_fusion.11), channel_id=1, source_target_pairs={{448,0},{464,16},{480,32},{496,48},{0,64},{16,80},{32,96},{48,112}... | collective-permute-start | bytes 200 | tf_op jit(solution)/shard_map/ppermute | solution.py:19
  82.0 9.1 %collective-permute-start.34 = (s32[8]{0:T(128)S(1)}, s32[8]{0:T(128)S(1)}, u32[]{:S(2)}, u32[]{:S(2)}) collective-permute-start(s32[8]{0:T(128)S(1)} %collective-permute-done.28), channel_id=1, source_target_pairs={{1,0},{2,1},{3,2},{4,3},{5,4},{6,5},{7,6},{8,7},{9,8},{10,9},{11,1... | collective-permute-start | bytes 104 | tf_op jit(solution)/shard_map/ppermute | solution.py:19
  83.7 9.9 %collective-permute-start.33 = (s32[8]{0:T(128)S(1)}, s32[8]{0:T(128)S(1)}, u32[]{:S(2)}, u32[]{:S(2)}) collective-permute-start(s32[8]{0:T(128)S(1)} %collective-permute-done.27), channel_id=1, source_target_pairs={{1,0},{2,1},{3,2},{4,3},{5,4},{6,5},{7,6},{8,7},{9,8},{10,9},{11,1... | collective-permute-start | bytes 104 | tf_op jit(solution)/shard_map/ppermute | solution.py:19
  86.6 13.0 %collective-permute-start.15 = (s32[2,8]{1,0:T(2,128)S(1)}, s32[2,8]{1,0:T(2,128)S(1)}, u32[]{:S(2)}, u32[]{:S(2)}) collective-permute-start(s32[2,8]{1,0:T(2,128)S(1)} %broadcast_select_fusion.14), channel_id=1, source_target_pairs={{384,0},{400,16},{416,32},{432,48},{448,64},{464,80},{480,96},{496... | collective-permute-start | bytes 200 | tf_op jit(solution)/shard_map/ppermute | solution.py:19
  91.1 12.8 %collective-permute-start.20 = (s32[2,8]{1,0:T(2,128)S(1)}, s32[2,8]{1,0:T(2,128)S(1)}, u32[]{:S(2)}, u32[]{:S(2)}) collective-permute-start(s32[2,8]{1,0:T(2,128)S(1)} %broadcast_select_fusion.13), channel_id=1, source_target_pairs={{384,0},{400,16},{416,32},{432,48},{448,64},{464,80},{480,96},{496... | collective-permute-start | bytes 200 | tf_op jit(solution)/shard_map/ppermute | solution.py:19
  99.5 22.5 %collective-permute-start.16 = (s32[2,8]{1,0:T(2,128)S(1)}, s32[2,8]{1,0:T(2,128)S(1)}, u32[]{:S(2)}, u32[]{:S(2)}) collective-permute-start(s32[2,8]{1,0:T(2,128)S(1)} %broadcast_select_fusion.16), channel_id=1, source_target_pairs={{256,0},{272,16},{288,32},{304,48},{320,64},{336,80},{352,96},{368... | collective-permute-start | bytes 200 | tf_op jit(solution)/shard_map/ppermute | solution.py:19
  104.0 18.1 %collective-permute-start.21 = (s32[2,8]{1,0:T(2,128)S(1)}, s32[2,8]{1,0:T(2,128)S(1)}, u32[]{:S(2)}, u32[]{:S(2)}) collective-permute-start(s32[2,8]{1,0:T(2,128)S(1)} %broadcast_select_fusion.15), channel_id=1, source_target_pairs={{256,0},{272,16},{288,32},{304,48},{320,64},{336,80},{352,96},{368... | collective-permute-start | bytes 200 | tf_op jit(solution)/shard_map/ppermute | solution.py:19
  108.8 11.2 %collective-permute-start.9 = (bf16[8,128,128]{2,1,0:T(8,128)(2,1)S(1)}, bf16[8,128,128]{2,1,0:T(8,128)(2,1)S(1)}, u32[]{:S(2)}, u32[]{:S(2)}) collective-permute-start(bf16[8,128,128]{2,1,0:T(8,128)(2,1)S(1)} %broadcast_select_fusion.5), channel_id=1, source_target_pairs={{14,0},{15,1},{0,2},{1,3},{2,4},{3,5},{4,6},{5,7},{6,8},{7,9},{8,1... | collective-permute-start | bytes 786440 | tf_op jit(solution)/shard_map/ppermute | solution.py:19
  110.9 36.3 %collective-permute-start.23 = (bf16[2,8,128,128]{3,2,1,0:T(8,128)(2,1)S(1)}, bf16[2,8,128,128]{3,2,1,0:T(8,128)(2,1)S(1)}, u32[]{:S(2)}, u32[]{:S(2)}) collective-permute-start(bf16[2,8,128,128]{3,2,1,0:T(8,128)(2,1)S(1)} %broadcast_select_fusion), channel_id=1, source_target_pairs={{480,0},{496,16},{0,32},{16,48},{32,64},{48,80},{64,96},{80,112},{... | collective-permute-start | bytes 1572872 | tf_op jit(solution)/shard_map/ppermute | solution.py:19
  120.1 21.6 %collective-permute-start.10 = (bf16[8,128,128]{2,1,0:T(8,128)(2,1)S(1)}, bf16[8,128,128]{2,1,0:T(8,128)(2,1)S(1)}, u32[]{:S(2)}, u32[]{:S(2)}) collective-permute-start(bf16[8,128,128]{2,1,0:T(8,128)(2,1)S(1)} %broadcast_select_fusion.6), channel_id=1, source_target_pairs={{12,0},{13,1},{14,2},{15,3},{0,4},{1,5},{2,6},{3,7},{4,8},{5,9},{6... | collective-permute-start | bytes 786440 | tf_op jit(solution)/shard_map/ppermute | solution.py:19
  122.1 8.8 %collective-permute-start.31 = (s32[2,8]{1,0:T(2,128)S(1)}, s32[2,8]{1,0:T(2,128)S(1)}, u32[]{:S(2)}, u32[]{:S(2)}) collective-permute-start(s32[2,8]{1,0:T(2,128)S(1)} %get-tuple-element.7), channel_id=1, source_target_pairs={{32,0},{48,16},{64,32},{80,48},{96,64},{112,80},{128,96},{144,112}... | collective-permute-start | bytes 200 | tf_op jit(solution)/shard_map/ppermute | solution.py:19
  134.1 15.5 %collective-permute-start.37 = (s32[2,8]{1,0:T(2,128)S(1)}, s32[2,8]{1,0:T(2,128)S(1)}, u32[]{:S(2)}, u32[]{:S(2)}) collective-permute-start(s32[2,8]{1,0:T(2,128)S(1)} %collective-permute-done.31), channel_id=1, source_target_pairs={{32,0},{48,16},{64,32},{80,48},{96,64},{112,80},{128,96},{144,112}... | collective-permute-start | bytes 200 | tf_op jit(solution)/shard_map/ppermute | solution.py:19
  138.9 10.6 %collective-permute-start.36 = (s32[2,8]{1,0:T(2,128)S(1)}, s32[2,8]{1,0:T(2,128)S(1)}, u32[]{:S(2)}, u32[]{:S(2)}) collective-permute-start(s32[2,8]{1,0:T(2,128)S(1)} %collective-permute-done.30), channel_id=1, source_target_pairs={{32,0},{48,16},{64,32},{80,48},{96,64},{112,80},{128,96},{144,112}... | collective-permute-start | bytes 200 | tf_op jit(solution)/shard_map/ppermute | solution.py:19
  141.7 19.9 %collective-permute-start.11 = (bf16[8,128,128]{2,1,0:T(8,128)(2,1)S(1)}, bf16[8,128,128]{2,1,0:T(8,128)(2,1)S(1)}, u32[]{:S(2)}, u32[]{:S(2)}) collective-permute-start(bf16[8,128,128]{2,1,0:T(8,128)(2,1)S(1)} %broadcast_select_fusion.7), channel_id=1, source_target_pairs={{8,0},{9,1},{10,2},{11,3},{12,4},{13,5},{14,6},{15,7},{0,8},{1,9},... | collective-permute-start | bytes 786440 | tf_op jit(solution)/shard_map/ppermute | solution.py:19
  147.2 20.0 %collective-permute-start.24 = (bf16[2,8,128,128]{3,2,1,0:T(8,128)(2,1)S(1)}, bf16[2,8,128,128]{3,2,1,0:T(8,128)(2,1)S(1)}, u32[]{:S(2)}, u32[]{:S(2)}) collective-permute-start(bf16[2,8,128,128]{3,2,1,0:T(8,128)(2,1)S(1)} %broadcast_select_fusion.1), channel_id=1, source_target_pairs={{448,0},{464,16},{480,32},{496,48},{0,64},{16,80},{32,96},{48,112}... | collective-permute-start | bytes 1572872 | tf_op jit(solution)/shard_map/ppermute | solution.py:19
  161.6 8.8 %collective-permute-start.29 = (bf16[8,128,128]{2,1,0:T(8,128)(2,1)S(1)}, bf16[8,128,128]{2,1,0:T(8,128)(2,1)S(1)}, u32[]{:S(2)}, u32[]{:S(2)}) collective-permute-start(bf16[8,128,128]{2,1,0:T(8,128)(2,1)S(1)} %broadcast_select_fusion.8), channel_id=1, source_target_pairs={{1,0},{2,1},{3,2},{4,3},{5,4},{6,5},{7,6},{8,7},{9,8},{10,9},{11,1... | collective-permute-start | bytes 786440 | tf_op jit(solution)/shard_map/ppermute | solution.py:19
  167.3 26.0 %collective-permute-start.25 = (bf16[2,8,128,128]{3,2,1,0:T(8,128)(2,1)S(1)}, bf16[2,8,128,128]{3,2,1,0:T(8,128)(2,1)S(1)}, u32[]{:S(2)}, u32[]{:S(2)}) collective-permute-start(bf16[2,8,128,128]{3,2,1,0:T(8,128)(2,1)S(1)} %broadcast_select_fusion.2), channel_id=1, source_target_pairs={{384,0},{400,16},{416,32},{432,48},{448,64},{464,80},{480,96},{496... | collective-permute-start | bytes 1572872 | tf_op jit(solution)/shard_map/ppermute | solution.py:19
  176.6 21.5 %collective-permute-start.41 = (bf16[8,128,128]{2,1,0:T(8,128)(2,1)S(1)}, bf16[8,128,128]{2,1,0:T(8,128)(2,1)S(1)}, u32[]{:S(2)}, u32[]{:S(2)}) collective-permute-start(bf16[8,128,128]{2,1,0:T(8,128)(2,1)S(1)} %collective-permute-done.35), channel_id=1, source_target_pairs={{1,0},{2,1},{3,2},{4,3},{5,4},{6,5},{7,6},{8,7},{9,8},{10,9},{11,1... | collective-permute-start | bytes 786440 | tf_op jit(solution)/shard_map/ppermute | solution.py:19
  193.4 30.9 %collective-permute-start.26 = (bf16[2,8,128,128]{3,2,1,0:T(8,128)(2,1)S(1)}, bf16[2,8,128,128]{3,2,1,0:T(8,128)(2,1)S(1)}, u32[]{:S(2)}, u32[]{:S(2)}) collective-permute-start(bf16[2,8,128,128]{3,2,1,0:T(8,128)(2,1)S(1)} %broadcast_select_fusion.3), channel_id=1, source_target_pairs={{256,0},{272,16},{288,32},{304,48},{320,64},{336,80},{352,96},{368... | collective-permute-start | bytes 1572872 | tf_op jit(solution)/shard_map/ppermute | solution.py:19
  224.3 16.3 %collective-permute-start.32 = (bf16[2,8,128,128]{3,2,1,0:T(8,128)(2,1)S(1)}, bf16[2,8,128,128]{3,2,1,0:T(8,128)(2,1)S(1)}, u32[]{:S(2)}, u32[]{:S(2)}) collective-permute-start(bf16[2,8,128,128]{3,2,1,0:T(8,128)(2,1)S(1)} %broadcast_select_fusion.4), channel_id=1, source_target_pairs={{32,0},{48,16},{64,32},{80,48},{96,64},{112,80},{128,96},{144,112}... | collective-permute-start | bytes 1572872 | tf_op jit(solution)/shard_map/ppermute | solution.py:19
  240.7 15.4 %collective-permute-start.38 = (bf16[2,8,128,128]{3,2,1,0:T(8,128)(2,1)S(1)}, bf16[2,8,128,128]{3,2,1,0:T(8,128)(2,1)S(1)}, u32[]{:S(2)}, u32[]{:S(2)}) collective-permute-start(bf16[2,8,128,128]{3,2,1,0:T(8,128)(2,1)S(1)} %collective-permute-done.32), channel_id=1, source_target_pairs={{32,0},{48,16},{64,32},{80,48},{96,64},{112,80},{128,96},{144,112}... | collective-permute-start | bytes 1572872 | tf_op jit(solution)/shard_map/ppermute | solution.py:19
  256.1 16.0 %collective-permute-start.44 = (bf16[2,8,128,128]{3,2,1,0:T(8,128)(2,1)S(1)}, bf16[2,8,128,128]{3,2,1,0:T(8,128)(2,1)S(1)}, u32[]{:S(2)}, u32[]{:S(2)}) collective-permute-start(bf16[2,8,128,128]{3,2,1,0:T(8,128)(2,1)S(1)} %collective-permute-done.38), channel_id=1, source_target_pairs={{32,0},{48,16},{64,32},{80,48},{96,64},{112,80},{128,96},{144,112}... | collective-permute-start | bytes 1572872 | tf_op jit(solution)/shard_map/ppermute | solution.py:19
  (14 other events, 185.6 us)
